TPU v7x, 256 devices: a whole 4x4x8 slice. The times are simulated.
256 devices in a mesh: wa: 16 (over y_hi, z), dev: 16 (over y_lo, x, core).
Axes of the slice: x: 4, y: 4 (y_hi: 2, y_lo: 2; y = y_hi * 2 + y_lo), z: 8, core: 2. Of those that a mesh axis runs over, the one named last changes fastest.
Arguments:
- output_gradient: bfloat16 [2048, 8192], P('wa'), may hold values from -6 to 6
- down_weight: bfloat16 [28672, 8192], P('dev', 'wa'), may hold values from -0.03125 to 0.03125
- gate_preactivation: bfloat16 [2048, 28672], P('wa', 'dev'), may hold values from -6 to 6
- up_preactivation: bfloat16 [2048, 28672], P('wa', 'dev'), may hold values from -6 to 6
- adapter_down_factor: bfloat16 [16, 16, 28672], P(None, None, 'dev'), may hold values from -0.0625 to 0.0625
- adapter_up_factor: bfloat16 [16, 16, 8192], P(None, None, 'dev'), may hold values from -0.0625 to 0.0625
- tile_owner_adapter: int32 [128, 1], replicated, may hold values from 0 to 15
- tile_live_count: int32 [128], replicated, may hold values from 1 to 16
Outputs:
- grad_gate: bfloat16 [2048, 28672], P('wa', 'dev')
- grad_up: bfloat16 [2048, 28672], P('wa', 'dev')
- grad_a: float32 [16, 16, 28672], P('wa', None, 'dev')
- grad_b: float32 [16, 16, 8192], P('wa', None, 'dev')
Inputs may be any that keep to these rules, and one draw needn't show every extreme that they name: `tile_owner_adapter`: every one of the 16 adapters owns at least one tile.
All inputs are finite; a program needn't handle non-finite values.
Results may differ from a plain program's by a relative error of at most 0.013.
Values may be sent and summed in bfloat16 or wider, within the bound.
A program may use at most 128 MiB of HBM per device.

v0:
```python
import jax
import jax.numpy as jnp
from jax import lax
from jax.sharding import PartitionSpec as P

TILE = 16


def on_device(
    output_gradient,
    down_weight,
    gate_preactivation,
    up_preactivation,
    adapter_down_factor,
    adapter_up_factor,
    tile_owner_adapter,
    tile_live_count,
):
    wa_index = lax.axis_index("wa")
    dev_index = lax.axis_index("dev")
    token_rows = output_gradient.shape[0]
    hidden_local = down_weight.shape[0]
    wa_cols = down_weight.shape[1]
    shard_columns = adapter_up_factor.shape[2]
    adapter_list = adapter_down_factor.shape[0]
    adapter_rank_rows = adapter_down_factor.shape[1]
    tiles_local = token_rows // TILE
    own_adapter = lax.dynamic_slice_in_dim(
        tile_owner_adapter[:, 0], wa_index * tiles_local, tiles_local
    )
    own_live = lax.dynamic_slice_in_dim(tile_live_count, wa_index * tiles_local, tiles_local)
    row_adapter = jnp.repeat(own_adapter, TILE)
    position = jnp.arange(token_rows) % TILE
    live_rows = position < jnp.repeat(own_live, TILE)
    masked_rows = jnp.where(
        live_rows[:, None], output_gradient, jnp.zeros((), output_gradient.dtype)
    )
    gate_wide = gate_preactivation.astype(jnp.float32)
    up_wide = up_preactivation.astype(jnp.float32)
    hidden_state = (jax.nn.silu(gate_wide) * up_wide).astype(jnp.bfloat16)
    shard_piece = lax.all_gather(down_weight, "wa", axis=1, tiled=True)
    groups = shard_piece.shape[1] // wa_cols
    left = masked_rows.reshape(token_rows, groups, wa_cols)
    right = shard_piece.reshape(hidden_local, groups, wa_cols)
    partial_value = jnp.einsum("tkc,fkc->ktf", left, right, preferred_element_type=jnp.float32)
    rounded = lax.optimization_barrier(partial_value.astype(jnp.bfloat16))
    base_grad = jnp.sum(rounded.astype(jnp.float32), axis=0)
    selector = row_adapter[:, None] == jnp.arange(adapter_list, dtype=jnp.int32)[None, :]
    flattened_down = adapter_down_factor.reshape(adapter_list * adapter_rank_rows, hidden_local)
    flattened_up = adapter_up_factor.reshape(adapter_list * adapter_rank_rows, shard_columns)

    def choose_rows(complete_value):
        reshaped_value = complete_value.reshape(token_rows, adapter_list, adapter_rank_rows)
        return jnp.sum(
            jnp.where(selector[:, :, None], reshaped_value, jnp.zeros((), complete_value.dtype)),
            axis=1,
        )

    def spread_value(values):
        wide_value = jnp.where(
            selector[:, :, None], values[:, None, :], jnp.zeros((), values.dtype)
        )
        return wide_value.reshape(token_rows, adapter_list * adapter_rank_rows)

    grad_slice = lax.dynamic_slice_in_dim(masked_rows, dev_index * shard_columns, shard_columns, 1)
    in_partial = choose_rows(
        lax.dot_general(
            hidden_state,
            flattened_down,
            (((1,), (1,)), ((), ())),
            preferred_element_type=jnp.float32,
        )
    )
    out_partial = choose_rows(
        lax.dot_general(
            grad_slice, flattened_up, (((1,), (1,)), ((), ())), preferred_element_type=jnp.float32
        )
    )
    in_summed, out_summed = lax.psum((in_partial, out_partial), "dev")
    spread_input = spread_value(in_summed.astype(jnp.bfloat16))
    spread_output = spread_value(out_summed.astype(jnp.bfloat16))
    hidden_grad = base_grad + 2.0 * jnp.dot(
        spread_output, flattened_down, preferred_element_type=jnp.float32
    )
    sigmoid_gate = jax.nn.sigmoid(gate_wide)
    grad_up = (hidden_grad * gate_wide * sigmoid_gate).astype(jnp.bfloat16)
    grad_gate = (
        hidden_grad * up_wide * sigmoid_gate * (1.0 + gate_wide * (1.0 - sigmoid_gate))
    ).astype(jnp.bfloat16)
    down_factor_partial = 2.0 * lax.dot_general(
        spread_output, hidden_state, (((0,), (0,)), ((), ())), preferred_element_type=jnp.float32
    )
    up_factor_partial = 2.0 * lax.dot_general(
        spread_input, grad_slice, (((0,), (0,)), ((), ())), preferred_element_type=jnp.float32
    )
    down_factor_partial = down_factor_partial.reshape(adapter_list, adapter_rank_rows, hidden_local)
    up_factor_partial = up_factor_partial.reshape(adapter_list, adapter_rank_rows, shard_columns)
    grad_a, grad_b = (
        lax.psum_scatter(down_factor_partial, "wa", scatter_dimension=0, tiled=True),
        lax.psum_scatter(up_factor_partial, "wa", scatter_dimension=0, tiled=True),
    )
    return (grad_gate, grad_up, grad_a, grad_b)


def solution(mesh):
    placed = (
        P("wa", None),
        P("dev", "wa"),
        P("wa", "dev"),
        P("wa", "dev"),
        P(None, None, "dev"),
        P(None, None, "dev"),
        P(),
        P(),
    )
    return jax.shard_map(
        on_device,
        mesh=mesh,
        in_specs=placed,
        out_specs=(P("wa", "dev"), P("wa", "dev"), P("wa", None, "dev"), P("wa", None, "dev")),
        check_vma=False,
    )
```

profile of v0, /device:TPU:2, one launch (start us, length us, event | category | flops | bytes accessed | tf_op | source)
XLA Modules:
  0.0 798.2 jit_solution(14165972701911176698)
XLA Ops:
  7.2 0.0 all-gather.2.cloned.1.call-start
  7.2 3.9 copy.13
  11.2 0.0 all-gather.2.cloned.1.call-update
  11.2 0.0 reduce-scatter.5.cloned.1.call-start
  11.3 0.1 dynamic_slice.11
  11.3 0.1 broadcast_in_dim.69
  11.4 0.1 reshape.82
  11.5 0.1 dynamic-slice_bitcast_fusion
  11.6 0.1 broadcast_in_dim.72
  11.6 0.1 eq.21
  11.8 1.9 broadcast_select_fusion
  13.7 0.2 fusion.5
  14.0 0.5 fusion.4
  14.5 52.8 %all-reduce = (bf16[128,16]{0,1:T(8,128)(2,1)S(1)}, bf16[128,16]{0,1:T(8,128)(2,1)S(1)}) all-reduce(f32[128,16]{0,1:T(8,128)S(1)} %fusion.5, f32[128,16]{0,1:T(8,128)S(1)} %fusion.4), channel_id=1, replica_groups=mesh['wa'=16,'dev'=16] {'dev'}, use_global_device_ids=true, to_apply=%region_2.3 | all-reduce | flops 4096 | bytes 24576 | tf_op jit(solution)/shard_map/psum | solution.py:79
  67.3 1.0 convolution_multiply_fusion.1
  68.3 0.0 reduce-scatter.5.cloned.1.call-update
  68.4 0.0 reduce-scatter.3.cloned.1.call-start
  68.4 2.9 convolution_multiply_fusion
  71.3 308.6 %all-gather.2.cloned.1.call-done = bf16[1792,8192]{0,1:T(8,128)(2,1)} async-done(((bf16[1792,512]{0,1:T(8,128)(2,1)}), bf16[1792,8192]{0,1:T(8,128)(2,1)}) %all-gather.2.cloned.1.call-update) | async-done | bytes 29360144 | tf_op jit(solution)/shard_map/all_gather | solution.py:41
  379.9 16.4 %convolution_convert_fusion = bf16[16,128,1792]{2,1,0:T(8,128)(2,1)} fusion(bf16[1792,16,512]{0,2,1:T(8,128)(2,1)} %bitcast.29, bf16[16,16,8,512]{3,2,1,0:T(8,128)(2,1)S(1)} %bitcast.30), kind=kOutput, calls=%fused_computation.1 | convolution fusion | flops 3761766400 | bytes 38797312 | tf_op jit(solution)/shard_map/tkc,fkc->ktf/dot_general | solution.py:45
  396.3 4.3 convert_reduce_fusion
  400.6 1.6 fusion.15
  402.2 178.1 %reduce-scatter.5.cloned.1.call-done = f32[1,16,512]{2,1,0:T(8,128)} async-done(((f32[16,16,512]{2,1,0:T(8,128)}), f32[1,16,512]{2,1,0:T(8,128)}) %reduce-scatter.5.cloned.1.call-update) | async-done | bytes 32784 | tf_op jit(solution)/shard_map/reduce_scatter | solution.py:100
  580.3 211.3 %reduce-scatter.3.cloned.1.call-done = f32[1,16,1792]{2,1,0:T(8,128)} async-done(((f32[16,16,1792]{2,1,0:T(8,128)}), f32[1,16,1792]{2,1,0:T(8,128)}) %reduce-scatter.3.cloned.1.call-update) | async-done | bytes 114704 | tf_op jit(solution)/shard_map/reduce_scatter | solution.py:99
  (18 shorter events, 0.1 us)
Async XLA Ops:
  7.2 6.8 copy-start
  7.2 4.1 copy-start.5
  7.2 4.3 copy-start.6
  7.2 372.7 %all-gather.2.cloned.1.call-start = ((), (), s32[]{:S(2)}) async-start(), calls=%async_computation.2 | async-start | bytes 31195136 | tf_op jit(solution)/shard_map/all_gather | solution.py:41
  11.2 569.1 %reduce-scatter.5.cloned.1.call-start = ((), (), s32[]{:S(2)}) async-start(), calls=%async_computation.4 | async-start | bytes 557056 | tf_op jit(solution)/shard_map/reduce_scatter | solution.py:100
  11.7 1.9 copy-start.1
  11.8 2.2 copy-start.2
  11.8 2.2 copy-start.3
  68.4 723.3 %reduce-scatter.3.cloned.1.call-start = ((), (), s32[]{:S(2)}) async-start(), calls=%async_computation.3 | async-start | bytes 1949696 | tf_op jit(solution)/shard_map/reduce_scatter | solution.py:99
  396.3 4.3 copy-start.4
Sparse Core Ops, SparseCore 0:
  11.3 368.5 all-gather.1
  384.2 196.0 reduce-scatter.4
  584.8 206.8 reduce-scatter.2
where the time goes:
time: 798 us
  waiting for transfers between devices  698 us (87%)
  blocking collectives  52.8 us (7%)
  matrix products  22.7 us (3%)
  between operations  13.9 us (2%)
    all_gather x1, waiting for transfers between devices, on_device(): shard_piece = lax.all_gather(down_weight, 'wa', axis=1, tiled=True)  309 us
    reduce_scatter x1, waiting for transfers between devices, on_device(): lax.psum_scatter(down_factor_partial, 'wa', scatter_dimension=0, tiled=True)  211 us
    reduce_scatter x1, waiting for transfers between devices, on_device(): lax.psum_scatter(up_factor_partial, 'wa', scatter_dimension=0, tiled=True)  178 us
    psum x1, blocking collectives, on_device(): in_summed, out_summed = lax.psum((in_partial, out_partial), 'dev')  52.8 us
    dot_general x1, matrix products, on_device(): jnp.einsum('tkc,fkc->ktf', left, right, preferred_element_type=jnp.float32)  16.4 us
  transfers between devices with their start and end apart: 3, of which 3 were waited for; matrix products, arithmetic and copies ran while one was open for 4% of the time, Pallas kernels for 0%

commit v1 on v0

--- a/solution.py
+++ b/solution.py
@@ -38,7 +38,9 @@
     gate_wide = gate_preactivation.astype(jnp.float32)
     up_wide = up_preactivation.astype(jnp.float32)
     hidden_state = (jax.nn.silu(gate_wide) * up_wide).astype(jnp.bfloat16)
-    shard_piece = lax.all_gather(down_weight, "wa", axis=1, tiled=True)
+    shard_piece = jnp.concatenate(
+        lax.all_to_all(jnp.stack([down_weight] * lax.axis_size("wa")), "wa", 0, 0), axis=1
+    )
     groups = shard_piece.shape[1] // wa_cols
     left = masked_rows.reshape(token_rows, groups, wa_cols)
     right = shard_piece.reshape(hidden_local, groups, wa_cols)

time: 798 us -> 939 us (1.18)
  waiting for transfers between devices: 698 us -> 816 us
  starting transfers between devices: 0.12 us -> 11.5 us
    all_to_all x0 -> x1, waiting for transfers between devices: none -> 600 us  [on_device(): lax.all_to_all(jnp.stack([down_weight] * lax.axis_size('wa')), 'wa', 0, 0)]
    all_gather x1 -> x0, waiting for transfers between devices: 309 us -> none  [on_device(): shard_piece = lax.all_gather(down_weight, 'wa', axis=1, tiled=True)]
    reduce_scatter x1, waiting for transfers between devices: 178 us -> 0.01 us  [on_device(): lax.psum_scatter(up_factor_partial, 'wa', scatter_dimension=0, tiled=True)]
    all_to_all x0 -> x1, starting transfers between devices: none -> 11.4 us  [on_device(): lax.all_to_all(jnp.stack([down_weight] * lax.axis_size('wa')), 'wa', 0, 0)]
    another operation x0 -> x1, local copies, waits for them, and re-layouts: none -> 11 us  [on_device(): jnp.stack([down_weight] * lax.axis_size('wa'))]
  transfers between devices with their start and end apart: 3 -> 3, of which waited for: 3 -> 2; matrix products, arithmetic and copies ran while one was open for 4% -> 3% of each run, Pallas kernels for 0% -> 0%
where the time goes in v1:
time: 939 us; the launch traced here: 938 us
  waiting for transfers between devices  816 us (87%)
  blocking collectives  55.4 us (6%)
  matrix products  23.9 us (3%)
  between operations  14.2 us (2%)
  local copies, waits for them, and re-layouts  11.5 us (1%)
  starting transfers between devices  11.5 us (1%)
    all_to_all x1, waiting for transfers between devices, on_device(): lax.all_to_all(jnp.stack([down_weight] * lax.axis_size('wa')), 'wa', 0, 0)  600 us
    reduce_scatter x1, waiting for transfers between devices, on_device(): lax.psum_scatter(down_factor_partial, 'wa', scatter_dimension=0, tiled=True)  215 us
    psum x1, blocking collectives, on_device(): in_summed, out_summed = lax.psum((in_partial, out_partial), 'dev')  55.4 us
  transfers between devices with their start and end apart: 3, of which 2 were waited for; matrix products, arithmetic and copies ran while one was open for 3% of the time, Pallas kernels for 0%

profile of v1, /device:TPU:2, one launch (start us, length us, event | category | flops | bytes accessed | tf_op | source)
XLA Modules:
  0.0 938.4 jit_solution(10958148752287580725)
XLA Ops:
  7.2 0.0 copy-start
  7.2 11.0 %stack.2 = bf16[16,1792,512]{2,1,0:T(8,128)(2,1)} broadcast(bf16[1792,512]{1,0:T(8,128)(2,1)} %param.9), dimensions={1,2} | broadcast | bytes 31195136 | tf_op jit(solution)/shard_map/stack | solution.py:42
  18.2 11.4 %all-to-all-start = ((bf16[16,1792,512]{2,1,0:T(8,128)(2,1)}), bf16[16,1792,512]{2,1,0:T(8,128)(2,1)}, u32[]{:S(2)}, u32[]{:S(2)}) async-start(bf16[16,1792,512]{2,1,0:T(8,128)(2,1)} %stack.2), calls=%async_computation | async-start | bytes 58720256 | tf_op jit(solution)/shard_map/all_to_all | solution.py:42
  29.6 0.0 reduce-scatter.5.cloned.1.call-start
  29.7 0.1 dynamic_slice.11
  29.8 0.1 broadcast_in_dim.69
  29.8 0.1 reshape.84
  29.9 0.1 dynamic-slice_bitcast_fusion
  30.0 0.1 broadcast_in_dim.72
  30.1 0.1 eq.21
  30.2 1.9 broadcast_select_fusion
  32.1 0.2 fusion.10
  32.4 0.5 fusion.9
  32.9 55.4 %all-reduce = (bf16[128,16]{0,1:T(8,128)(2,1)S(1)}, bf16[128,16]{0,1:T(8,128)(2,1)S(1)}) all-reduce(f32[128,16]{0,1:T(8,128)S(1)} %fusion.10, f32[128,16]{0,1:T(8,128)S(1)} %fusion.9), channel_id=1, replica_groups=mesh['wa'=16,'dev'=16] {'dev'}, use_global_device_ids=true, to_apply=%region_2.3 | all-reduce | flops 4096 | bytes 24576 | tf_op jit(solution)/shard_map/psum | solution.py:81
  88.4 1.1 convolution_multiply_fusion.1
  89.4 0.0 reduce-scatter.5.cloned.1.call-update
  89.4 0.0 reduce-scatter.3.cloned.1.call-start
  89.5 2.8 convolution_multiply_fusion
  92.3 0.0 reduce-scatter.3.cloned.1.call-update
  92.3 600.5 %all-to-all-done = bf16[16,1792,512]{2,1,0:T(8,128)(2,1)} async-done(((bf16[16,1792,512]{2,1,0:T(8,128)(2,1)}), bf16[16,1792,512]{2,1,0:T(8,128)(2,1)}, u32[]{:S(2)}, u32[]{:S(2)}) %all-to-all-start) | async-done | bytes 29360160 | tf_op jit(solution)/shard_map/all_to_all | solution.py:42
  692.8 17.7 %fusion.2 = bf16[16,128,1792]{2,1,0:T(8,128)(2,1)} fusion(bf16[16,1792,512]{2,1,0:T(8,128)(2,1)} %all-to-all-done, bf16[16,16,8,512]{3,2,1,0:T(8,128)(2,1)S(1)} %bitcast.32), kind=kOutput, calls=%fused_computation.3 | convolution fusion | flops 3761766400 | bytes 38797312 | tf_op jit(solution)/shard_map/tkc,fkc->ktf/dot_general | solution.py:47
  710.5 4.3 convert_reduce_fusion
  714.8 1.6 fusion.20
  716.4 215.2 %reduce-scatter.3.cloned.1.call-done = f32[1,16,1792]{2,1,0:T(8,128)} async-done(((f32[16,16,1792]{2,1,0:T(8,128)}), f32[1,16,1792]{2,1,0:T(8,128)}) %reduce-scatter.3.cloned.1.call-update) | async-done | bytes 114704 | tf_op jit(solution)/shard_map/reduce_scatter | solution.py:101
  (17 shorter events, 0.1 us)
Async XLA Ops:
  7.2 25.2 %copy-start = (bf16[16,16,1792]{2,1,0:T(8,128)(2,1)S(1)}, bf16[16,16,1792]{2,1,0:T(8,128)(2,1)}, u32[]{:S(2)}) copy-start(bf16[16,16,1792]{2,1,0:T(8,128)(2,1)} %param.12) | copy-start | bytes 2752516
  18.2 11.5 %copy-start.5 = (s32[128]{0:T(128)S(1)}, s32[128]{0:T(128)}, u32[]{:S(2)}) copy-start(s32[128]{0:T(128)} %param.15) | copy-start | bytes 1540
  18.2 11.7 %copy-start.6 = (s32[128,1]{0,1:T(1,128)S(1)}, s32[128,1]{0,1:T(1,128)}, u32[]{:S(2)}) copy-start(s32[128,1]{0,1:T(1,128)} %param.14) | copy-start | bytes 1540
  18.2 674.6 %all-to-all-start = ((bf16[16,1792,512]{2,1,0:T(8,128)(2,1)}), bf16[16,1792,512]{2,1,0:T(8,128)(2,1)}, u32[]{:S(2)}, u32[]{:S(2)}) async-start(bf16[16,1792,512]{2,1,0:T(8,128)(2,1)} %stack.2), calls=%async_computation | async-start | bytes 58720256 | tf_op jit(solution)/shard_map/all_to_all | solution.py:42
  29.6 686.8 %reduce-scatter.5.cloned.1.call-start = ((), (), s32[]{:S(2)}) async-start(), calls=%async_computation.4 | async-start | bytes 557056 | tf_op jit(solution)/shard_map/reduce_scatter | solution.py:102
  30.2 1.9 copy-start.1
  30.2 2.2 copy-start.2
  30.2 2.2 copy-start.3
  89.4 842.1 %reduce-scatter.3.cloned.1.call-start = ((), (), s32[]{:S(2)}) async-start(), calls=%async_computation.3 | async-start | bytes 1949696 | tf_op jit(solution)/shard_map/reduce_scatter | solution.py:101
  710.5 4.3 copy-start.4
Sparse Core Ops, SparseCore 0:
  89.6 619.3 reduce-scatter.4
  713.4 218.1 reduce-scatter.2
